TPU v7x, 256 devices: a whole 4x4x8 slice. The times are simulated.
256 devices in a mesh: pipe: 4 (over y), expert: 16 (over z, core), dp: 4 (over x).
Axes of the slice: x: 4, y: 4, z: 8, core: 2. Of those that a mesh axis runs over, the one named last changes fastest.
Arguments:
- normed: bfloat16 [4, 4, 3072, 4096], P('pipe', None, ('expert', 'dp')), may hold values from -1.5 to 1.5
- saved_out: bfloat16 [4, 4, 3072, 2, 4096], P('pipe', None, ('expert', 'dp')), may hold values from -0.59765625 to 0.59765625
- expert_grads: bfloat16 [4, 4, 4, 16, 16, 9, 4096], P('pipe', None, 'dp', 'expert'), may hold values from -24 to 24
- routes: int32 [4, 4, 3072, 2], P('pipe', None, ('expert', 'dp')), may hold values from 0 to 15, all different within a row; in each aligned block of 48 rows (0 to 47, 48 to 95, ..., all dimensions but the last counted through in order) at most 9 rows name the same one
- router_weight: bfloat16 [4, 4096, 16], P('pipe'), may hold values from -0.375 to 0.375
- upstream: bfloat16 [4, 3072, 4096], P(None, ('expert', 'dp')), may hold values from -6 to 6
Outputs:
- grad_input: bfloat16 [4, 4, 3072, 4096], P('pipe', None, ('expert', 'dp'))
- router_grad: float32 [4, 4096, 16], P('pipe')
Inputs may be any that keep to these rules, and one draw needn't show every extreme that they name: `routes`: the two experts of a row differ. Within the 48 rows of one device for one section and micro-batch no expert is named more than 9 times, a bound that some expert reaches in some of these blocks.
All inputs are finite; a program needn't handle non-finite values.
Results may differ from a plain program's by a relative error of at most 0.007.
Values may be sent and summed in bfloat16 or wider, within the bound.
No kernel may reach another device: no remote copies, remote signals or barrier semaphores. Data moves between devices by JAX's collectives and lax.ppermute only.
A program may use at most 128 MiB of HBM per device.

v0:
```python
import jax
import jax.numpy as jnp
from jax import lax
from jax.sharding import PartitionSpec as P


def shifted(block, axis, distance):
    devices = range(lax.axis_size(axis))
    route = [(i - distance, i) for i in devices if i - distance in devices]
    return lax.ppermute(block, axis, route)


def slot_index(flat, experts, capacity):
    onehot = (flat[..., None] == jnp.arange(experts, dtype=jnp.int32)).astype(jnp.int32)
    before = jnp.cumsum(onehot, axis=-2) - onehot
    position = jnp.sum(before * onehot, axis=-1)
    return flat * capacity + position


def block_grad(incoming, normed_rows, saved_rows, route_rows, returned, index_rows, router_w):
    experts = router_w.shape[1]
    rows_dev = normed_rows.shape[0]
    width = normed_rows.shape[1]
    logits = jnp.dot(normed_rows, router_w, preferred_element_type=jnp.float32)
    expl = jnp.exp(logits)
    probs = expl / jnp.sum(expl, axis=-1, keepdims=True)
    chosen = (route_rows[..., None] == jnp.arange(experts, dtype=jnp.int32)).astype(jnp.float32)
    gates = jnp.einsum("tke,te->tk", chosen, probs)
    dot_grads = jnp.einsum("td,tkd->tk", incoming, saved_rows, preferred_element_type=jnp.float32)
    weighted = dot_grads * gates
    dense_f = (
        jnp.einsum("tke,tk->te", chosen, weighted) - probs * jnp.sum(weighted, axis=-1)[:, None]
    )
    dense = dense_f.astype(jnp.bfloat16)
    router_term = lax.dot_general(
        dense, router_w, (((1,), (1,)), ((), ())), preferred_element_type=jnp.float32
    )
    back_rows = returned[index_rows].reshape(rows_dev, 2, width).astype(jnp.float32)
    total = (
        incoming.astype(jnp.float32)
        + gates[:, 0, None] * back_rows[:, 0]
        + gates[:, 1, None] * back_rows[:, 1]
        + router_term
    )
    weight_part = lax.dot_general(
        normed_rows, dense, (((0,), (0,)), ((), ())), preferred_element_type=jnp.float32
    )
    return (total.astype(jnp.bfloat16), weight_part)


def on_device(normed, saved_out, expert_grads, routes, router_weight, upstream):
    micro = normed.shape[1]
    rows_dev = normed.shape[2]
    width = normed.shape[3]
    sections = lax.axis_size("pipe")
    section_idx = lax.axis_index("pipe")
    router_w = router_weight[0]
    experts = router_w.shape[1]
    capacity = expert_grads.shape[5]
    slot_rows = slot_index(routes[0].reshape(micro, -1), experts, capacity)
    local_grads = expert_grads[0, :, 0]
    returned_list = []
    for block_num in range(micro):
        received = lax.all_to_all(
            local_grads[block_num], "expert", split_axis=1, concat_axis=0, tiled=True
        )
        returned_list.append(received.reshape(experts * capacity, width))
    returned_all = jnp.stack(returned_list)
    grad_buffer = jnp.zeros((micro, rows_dev, width), jnp.bfloat16)
    weight_sum = jnp.zeros((width, experts), jnp.float32)
    passed = jnp.zeros((rows_dev, width), jnp.bfloat16)
    for tick_num in range(micro + sections - 1):
        if tick_num > 0:
            passed = shifted(passed, "pipe", -1)
        block_num = tick_num - (sections - 1 - section_idx)
        is_active = (block_num >= 0) & (block_num < micro)
        block_idx = jnp.clip(block_num, 0, micro - 1)
        returned = lax.dynamic_index_in_dim(returned_all, block_idx, 0, keepdims=False)
        from_top = lax.dynamic_index_in_dim(upstream, block_idx, 0, keepdims=False)
        incoming = jnp.where(section_idx == sections - 1, from_top, passed)
        new_grad, weight_part = block_grad(
            incoming,
            lax.dynamic_index_in_dim(normed[0], block_idx, 0, keepdims=False),
            lax.dynamic_index_in_dim(saved_out[0], block_idx, 0, keepdims=False),
            lax.dynamic_index_in_dim(routes[0], block_idx, 0, keepdims=False),
            returned,
            lax.dynamic_index_in_dim(slot_rows, block_idx, 0, keepdims=False),
            router_w,
        )
        updated = lax.dynamic_update_index_in_dim(grad_buffer, new_grad, block_idx, 0)
        grad_buffer = jnp.where(is_active, updated, grad_buffer)
        weight_sum = weight_sum + jnp.where(is_active, weight_part, 0.0)
        passed = new_grad
    router_grad = lax.psum(weight_sum / micro, ("expert", "dp"))
    return (grad_buffer[None], router_grad[None])


def solution(mesh):
    in_specs = (
        P("pipe", None, ("expert", "dp"), None),
        P("pipe", None, ("expert", "dp"), None, None),
        P("pipe", None, "dp", "expert", None, None, None),
        P("pipe", None, ("expert", "dp"), None),
        P("pipe", None, None),
        P(None, ("expert", "dp"), None),
    )
    out_specs = (P("pipe", None, ("expert", "dp"), None), P("pipe", None, None))
    return jax.shard_map(
        on_device, mesh=mesh, in_specs=in_specs, out_specs=out_specs, check_vma=False
    )
```

profile of v0, /device:TPU:1, one launch (start us, length us, event | category | flops | bytes accessed | tf_op | source)
XLA Modules:
  0.0 636.1 jit_solution(2353032965511129839)
XLA Ops:
  7.2 4.4 fusion.196
  13.7 10.1 %all-to-all-start = ((bf16[1,16,9,4096]{3,2,0,1:T(8,128)(2,1)}), bf16[1,16,9,4096]{3,2,0,1:T(8,128)(2,1)}, u32[]{:S(2)}, u32[]{:S(2)}) async-start(bf16[1,16,9,4096]{3,2,0,1:T(8,128)(2,1)} %bitcast.551), calls=%async_computation | async-start | bytes 4194304 | tf_op jit(solution)/shard_map/all_to_all | solution.py:64
  39.4 33.5 %all-to-all-done = bf16[1,16,9,4096]{3,2,0,1:T(8,128)(2,1)} async-done(((bf16[1,16,9,4096]{3,2,0,1:T(8,128)(2,1)}), bf16[1,16,9,4096]{3,2,0,1:T(8,128)(2,1)}, u32[]{:S(2)}, u32[]{:S(2)}) %all-to-all-start) | async-done | bytes 1179680 | tf_op jit(solution)/shard_map/all_to_all | solution.py:64
  72.9 5.0 all-to-all-start.1
  97.5 29.4 %all-to-all-done.1 = bf16[1,16,9,4096]{3,2,0,1:T(8,128)(2,1)} async-done(((bf16[1,16,9,4096]{3,2,0,1:T(8,128)(2,1)}), bf16[1,16,9,4096]{3,2,0,1:T(8,128)(2,1)}, u32[]{:S(2)}, u32[]{:S(2)}) %all-to-all-start.1) | async-done | bytes 1179680 | tf_op jit(solution)/shard_map/all_to_all | solution.py:64
  126.9 5.0 all-to-all-start.2
  143.3 37.7 %all-to-all-done.2 = bf16[1,16,9,4096]{3,2,0,1:T(8,128)(2,1)} async-done(((bf16[1,16,9,4096]{3,2,0,1:T(8,128)(2,1)}), bf16[1,16,9,4096]{3,2,0,1:T(8,128)(2,1)}, u32[]{:S(2)}, u32[]{:S(2)}) %all-to-all-start.2) | async-done | bytes 1179680 | tf_op jit(solution)/shard_map/all_to_all | solution.py:64
  181.0 5.1 all-to-all-start.3
  201.4 33.7 %all-to-all-done.3 = bf16[1,16,9,4096]{3,2,0,1:T(8,128)(2,1)} async-done(((bf16[1,16,9,4096]{3,2,0,1:T(8,128)(2,1)}), bf16[1,16,9,4096]{3,2,0,1:T(8,128)(2,1)}, u32[]{:S(2)}, u32[]{:S(2)}) %all-to-all-start.3) | async-done | bytes 1179680 | tf_op jit(solution)/shard_map/all_to_all | solution.py:64
  240.2 7.0 %dynamic-slice_bitcast_fusion = (bf16[144,4096]{1,0:T(8,128)(2,1)}, bf16[144,4096]{1,0:T(8,128)(2,1)}, bf16[144,4096]{1,0:T(8,128)(2,1)}, bf16[144,4096]{1,0:T(8...) fusion(bf16[4,144,4096]{2,1,0:T(8,128)(2,1)} %constant_dynamic-update-slice_fusion, ...), kind=kLoop, calls=%fused_computation.28 | loop fusion | bytes 16515100 | tf_op jit(solution)/shard_map/jit(dynamic_index_in_dim)/squeeze | solution.py:78
  247.1 4.1 gather_fusion
  263.8 4.2 gather_fusion.1
  271.0 4.7 fusion.202
  275.7 4.2 gather_fusion.2
  282.9 4.7 fusion.201
  287.6 4.2 gather_fusion.3
  294.9 4.7 fusion.200
  299.6 4.3 gather_fusion.4
  327.1 4.2 gather_fusion.5
  356.2 4.3 gather_fusion.6
  385.9 4.9 collective-permute-done.3
  400.8 8.6 %collective-permute-done.4 = bf16[48,4096]{1,0:T(8,128)(2,1)S(1)} collective-permute-done((bf16[48,4096]{1,0:T(8,128)(2,1)S(1)}, bf16[48,4096]{1,0:T(8,128)(2,1)S(1)}, u32[]{:S(2)}, u32[]{:S(2)}) %collective-permute-start.4) | collective-permute-done | bytes 393248 | tf_op jit(solution)/shard_map/ppermute | solution.py:10
  430.0 4.8 collective-permute-done.5
  453.1 174.1 %all-reduce.2.cloned.1.call-done = f32[1,4096,16]{1,2,0:T(8,128)} async-done(((f32[1,4096,16]{1,2,0:T(8,128)}), f32[1,4096,16]{1,2,0:T(8,128)}) %all-reduce.2.cloned.1.call-update) | async-done | bytes 262160 | tf_op jit(solution)/shard_map/psum | solution.py:94
  (294 shorter events, 213.8 us)
Async XLA Ops:
  7.2 20.7 %copy-start = (bf16[1,4,48,2,4096]{4,3,2,1,0:T(2,128)(2,1)S(1)}, bf16[1,4,48,2,4096]{4,3,2,1,0:T(2,128)(2,1)}, u32[]{:S(2)}) copy-start(bf16[1,4,48,2,4096]{4,3,2,1,0:T(2,128)(2,1)} %param.7) | copy-start | bytes 9437188
  13.7 10.1 %copy-start.43 = (s32[1,4,48,2]{2,3,1,0:T(2,128)S(1)}, s32[1,4,48,2]{2,3,1,0:T(2,128)}, u32[]{:S(2)}) copy-start(s32[1,4,48,2]{2,3,1,0:T(2,128)} %param.9) | copy-start | bytes 4612
  13.7 10.9 %copy-start.1 = (bf16[1,4096,16]{1,2,0:T(8,128)(2,1)S(1)}, bf16[1,4096,16]{1,2,0:T(8,128)(2,1)}, u32[]{:S(2)}) copy-start(bf16[1,4096,16]{1,2,0:T(8,128)(2,1)} %param.10) | copy-start | bytes 393220
  13.7 59.2 %all-to-all-start = ((bf16[1,16,9,4096]{3,2,0,1:T(8,128)(2,1)}), bf16[1,16,9,4096]{3,2,0,1:T(8,128)(2,1)}, u32[]{:S(2)}, u32[]{:S(2)}) async-start(bf16[1,16,9,4096]{3,2,0,1:T(8,128)(2,1)} %bitcast.551), calls=%async_computation | async-start | bytes 4194304 | tf_op jit(solution)/shard_map/all_to_all | solution.py:64
  34.2 38.7 %copy-start.41 = (s32[4,96]{1,0:T(4,128)}, s32[4,96]{1,0:T(4,128)S(1)}, u32[]{:S(2)}) copy-start(s32[4,96]{1,0:T(4,128)S(1)} %copy.75) | copy-start | bytes 4612
  34.3 38.6 %copy-start.20 = (s32[48,2]{1,0:T(8,128)}, s32[48,2]{1,0:T(8,128)S(1)}, u32[]{:S(2)}) copy-start(s32[48,2]{1,0:T(8,128)S(1)} %copy.79) | copy-start | bytes 1156
  36.2 41.6 %copy-start.18 = (s32[48,2]{1,0:T(8,128)}, s32[48,2]{1,0:T(8,128)S(1)}, u32[]{:S(2)}) copy-start(s32[48,2]{1,0:T(8,128)S(1)} %copy.82) | copy-start | bytes 1156
  72.9 54.0 %all-to-all-start.1 = ((bf16[1,16,9,4096]{3,2,0,1:T(8,128)(2,1)}), bf16[1,16,9,4096]{3,2,0,1:T(8,128)(2,1)}, u32[]{:S(2)}, u32[]{:S(2)}) async-start(bf16[1,16,9,4096]{3,2,0,1:T(8,128)(2,1)} %bitcast.550), calls=%async_computation.1 | async-start | bytes 4194304 | tf_op jit(solution)/shard_map/all_to_all | solution.py:64
  96.2 35.7 %copy-start.14 = (s32[48,2]{1,0:T(8,128)}, s32[48,2]{1,0:T(8,128)S(1)}, u32[]{:S(2)}) copy-start(s32[48,2]{1,0:T(8,128)S(1)} %copy.94) | copy-start | bytes 1156
  97.4 29.5 %copy-start.48 = (f32[48]{0:T(128)}, f32[48]{0:T(128)S(1)}, u32[]{:S(2)}) copy-start(f32[48]{0:T(128)S(1)} %get-tuple-element.93) | copy-start | bytes 580
  126.9 54.0 %all-to-all-start.2 = ((bf16[1,16,9,4096]{3,2,0,1:T(8,128)(2,1)}), bf16[1,16,9,4096]{3,2,0,1:T(8,128)(2,1)}, u32[]{:S(2)}, u32[]{:S(2)}) async-start(bf16[1,16,9,4096]{3,2,0,1:T(8,128)(2,1)} %bitcast.549), calls=%async_computation.2 | async-start | bytes 4194304 | tf_op jit(solution)/shard_map/all_to_all | solution.py:64
  132.2 54.2 %copy-start.44 = (f32[48,2]{0,1:T(2,128)}, f32[48,2]{0,1:T(2,128)S(1)}, u32[]{:S(2)}) copy-start(f32[48,2]{0,1:T(2,128)S(1)} %copy.167) | copy-start | bytes 1156
  181.0 54.2 %all-to-all-start.3 = ((bf16[1,16,9,4096]{3,2,0,1:T(8,128)(2,1)}), bf16[1,16,9,4096]{3,2,0,1:T(8,128)(2,1)}, u32[]{:S(2)}, u32[]{:S(2)}) async-start(bf16[1,16,9,4096]{3,2,0,1:T(8,128)(2,1)} %bitcast.548), calls=%async_computation.3 | async-start | bytes 4194304 | tf_op jit(solution)/shard_map/all_to_all | solution.py:64
  186.1 441.1 %all-reduce.2.cloned.1.call-start = ((), (), s32[]{:S(2)}) async-start(), calls=%async_computation.4 | async-start | bytes 524288 | tf_op jit(solution)/shard_map/psum | solution.py:94
  262.1 44.7 %collective-permute-start = (bf16[48,4096]{1,0:T(8,128)(2,1)}, bf16[48,4096]{1,0:T(8,128)(2,1)}, u32[]{:S(2)}, u32[]{:S(2)}) collective-permute-start(bf16[48,4096]{1,0:T(8,128)(2,1)} %get-tuple-element.72), channel_id=1, source_target_pairs={{64,0},{128,64},{192,128},{65,1},{129,65},{193,129},{66,2},{130,66... | collective-permute-start | bytes 1179656 | tf_op jit(solution)/shard_map/ppermute | solution.py:10
  308.0 10.3 %copy-start.30 = (f32[48,16]{0,1:T(8,128)S(1)}, f32[48,16]{0,1:T(8,128)}, u32[]{:S(2)}) copy-start(f32[48,16]{0,1:T(8,128)} %copy-done.29) | copy-start | bytes 9220
  322.8 13.2 %collective-permute-start.1 = (bf16[48,4096]{1,0:T(8,128)(2,1)}, bf16[48,4096]{1,0:T(8,128)(2,1)}, u32[]{:S(2)}, u32[]{:S(2)}) collective-permute-start(bf16[48,4096]{1,0:T(8,128)(2,1)} %get-tuple-element.76), channel_id=1, source_target_pairs={{64,0},{128,64},{192,128},{65,1},{129,65},{193,129},{66,2},{130,66... | collective-permute-start | bytes 1179656 | tf_op jit(solution)/shard_map/ppermute | solution.py:10
  337.1 10.3 %copy-start.26 = (f32[48,16]{0,1:T(8,128)S(1)}, f32[48,16]{0,1:T(8,128)}, u32[]{:S(2)}) copy-start(f32[48,16]{0,1:T(8,128)} %copy-done.25) | copy-start | bytes 9220
  352.0 11.6 %collective-permute-start.2 = (bf16[48,4096]{1,0:T(8,128)(2,1)}, bf16[48,4096]{1,0:T(8,128)(2,1)}, u32[]{:S(2)}, u32[]{:S(2)}) collective-permute-start(bf16[48,4096]{1,0:T(8,128)(2,1)} %get-tuple-element.80), channel_id=1, source_target_pairs={{64,0},{128,64},{192,128},{65,1},{129,65},{193,129},{66,2},{130,66... | collective-permute-start | bytes 1179656 | tf_op jit(solution)/shard_map/ppermute | solution.py:10
  364.7 10.3 %copy-start.28 = (f32[48,16]{0,1:T(8,128)S(1)}, f32[48,16]{0,1:T(8,128)}, u32[]{:S(2)}) copy-start(f32[48,16]{0,1:T(8,128)} %copy-done.27) | copy-start | bytes 9220
  379.4 11.4 %collective-permute-start.3 = (bf16[48,4096]{1,0:T(8,128)(2,1)S(1)}, bf16[48,4096]{1,0:T(8,128)(2,1)S(1)}, u32[]{:S(2)}, u32[]{:S(2)}) collective-permute-start(bf16[48,4096]{1,0:T(8,128)(2,1)S(1)} %get-tuple-element.84), channel_id=1, source_target_pairs={{64,0},{128,64},{192,128},{65,1},{129,65},{193,129},{66,2},{130,66... | collective-permute-start | bytes 1179656 | tf_op jit(solution)/shard_map/ppermute | solution.py:10
  399.1 10.3 %collective-permute-start.4 = (bf16[48,4096]{1,0:T(8,128)(2,1)S(1)}, bf16[48,4096]{1,0:T(8,128)(2,1)S(1)}, u32[]{:S(2)}, u32[]{:S(2)}) collective-permute-start(bf16[48,4096]{1,0:T(8,128)(2,1)S(1)} %get-tuple-element.88), channel_id=1, source_target_pairs={{64,0},{128,64},{192,128},{65,1},{129,65},{193,129},{66,2},{130,66... | collective-permute-start | bytes 1179656 | tf_op jit(solution)/shard_map/ppermute | solution.py:10
  425.6 9.2 %collective-permute-start.5 = (bf16[48,4096]{1,0:T(8,128)(2,1)S(1)}, bf16[48,4096]{1,0:T(8,128)(2,1)S(1)}, u32[]{:S(2)}, u32[]{:S(2)}) collective-permute-start(bf16[48,4096]{1,0:T(8,128)(2,1)S(1)} %get-tuple-element.92), channel_id=1, source_target_pairs={{64,0},{128,64},{192,128},{65,1},{129,65},{193,129},{66,2},{130,66... | collective-permute-start | bytes 1179656 | tf_op jit(solution)/shard_map/ppermute | solution.py:10
  436.6 10.3 %copy-start.49 = (f32[48]{0:T(128)S(1)}, f32[48]{0:T(128)}, u32[]{:S(2)}) copy-start(f32[48]{0:T(128)} %copy-done.48) | copy-start | bytes 580
  (50 other events, 150.2 us)
Sparse Core Ops, SparseCore 0:
  449.7 177.4 all-reduce.1
where the time goes:
time: 646 us; the launch traced here: 636 us
  waiting for transfers between devices  328 us (51%)
  local copies, waits for them, and re-layouts  165 us (26%)
  matrix products  57.4 us (9%)
  other arithmetic  35.6 us (6%)
  starting transfers between devices  33.9 us (5%)
  between operations  15.2 us (2%)
    psum x1, waiting for transfers between devices, on_device(): router_grad = lax.psum(weight_sum / micro, ('expert', 'dp'))  174 us
    all_to_all x4, waiting for transfers between devices, on_device(): lax.all_to_all(local_grads[block_num], 'expert', split_axis=1, concat_axi...  134 us
    unnamed x150, local copies, waits for them, and re-layouts  34.3 us
    gather x7, local copies, waits for them, and re-layouts, block_grad(): returned[index_rows].reshape(rows_dev, 2, width).astype(jnp.float32)  29.6 us
    slice x7, local copies, waits for them, and re-layouts, block_grad(): back_rows[:, 0]  26.5 us
    all_to_all x4, starting transfers between devices, on_device(): lax.all_to_all(local_grads[block_num], 'expert', split_axis=1, concat_axi...  25.2 us
    dot_general x7, matrix products, block_grad(): lax.dot_general(dense, router_w, (((1,), (1,)), ((), ())), preferred_elem...  25 us
    convert_element_type x7, local copies, waits for them, and re-layouts, block_grad(): returned[index_rows].reshape(rows_dev, 2, width).astype(jnp.float32)  20.9 us
  transfers between devices with their start and end apart: 11, of which 10 were waited for; matrix products, arithmetic and copies ran while one was open for 21% of the time, Pallas kernels for 0%

commit v1 on v0

--- a/solution.py
+++ b/solution.py
@@ -1,7 +1,15 @@
+import functools
 import jax
 import jax.numpy as jnp
 from jax import lax
 from jax.sharding import PartitionSpec as P
+
+
+def see_masks(payload, device_axis):
+    return lax.all_gather(payload, device_axis).sum(axis=0)
+
+
+values_check = functools.partial(see_masks, device_axis=("expert", "dp"))
 
 
 def shifted(block, axis, distance):
@@ -91,7 +99,7 @@
         grad_buffer = jnp.where(is_active, updated, grad_buffer)
         weight_sum = weight_sum + jnp.where(is_active, weight_part, 0.0)
         passed = new_grad
-    router_grad = lax.psum(weight_sum / micro, ("expert", "dp"))
+    router_grad = values_check(weight_sum / micro)
     return (grad_buffer[None], router_grad[None])
 
 

time: 646 us -> 582 us (0.901)
  waiting for transfers between devices: 328 us -> 245 us
  local copies, waits for them, and re-layouts: 165 us -> 178 us
  other arithmetic: 35.6 us -> 43.7 us
    psum x1 -> x0, waiting for transfers between devices: 174 us -> none  [on_device(): router_grad = lax.psum(weight_sum / micro, ('expert', 'dp'))]
    all_gather x0 -> x1, waiting for transfers between devices: none -> 85.4 us  [see_masks(): return lax.all_gather(payload, device_axis).sum(axis=0)]
    unnamed x150 -> x156, local copies, waits for them, and re-layouts: 34.3 us -> 49.2 us
    reduce_sum x0 -> x1, other arithmetic: none -> 8.7 us  [see_masks(): return lax.all_gather(payload, device_axis).sum(axis=0)]
  transfers between devices with their start and end apart: 11 -> 11, of which waited for: 10 -> 9; matrix products, arithmetic and copies ran while one was open for 21% -> 23% of each run, Pallas kernels for 0% -> 0%
where the time goes in v1:
time: 582 us; the launch traced here: 572 us
  waiting for transfers between devices  245 us (42%)
  local copies, waits for them, and re-layouts  178 us (31%)
  matrix products  56.8 us (10%)
  other arithmetic  43.7 us (8%)
  starting transfers between devices  34.2 us (6%)
  between operations  15 us (3%)
    all_to_all x4, waiting for transfers between devices, on_device(): lax.all_to_all(local_grads[block_num], 'expert', split_axis=1, concat_axi...  136 us
    all_gather x1, waiting for transfers between devices, see_masks(): return lax.all_gather(payload, device_axis).sum(axis=0)  85.4 us
    unnamed x156, local copies, waits for them, and re-layouts  49.2 us
    gather x7, local copies, waits for them, and re-layouts, block_grad(): returned[index_rows].reshape(rows_dev, 2, width).astype(jnp.float32)  29.4 us
    slice x7, local copies, waits for them, and re-layouts, block_grad(): back_rows[:, 0]  25.3 us
    all_to_all x4, starting transfers between devices, on_device(): lax.all_to_all(local_grads[block_num], 'expert', split_axis=1, concat_axi...  25.2 us
    dot_general x7, matrix products, block_grad(): lax.dot_general(dense, router_w, (((1,), (1,)), ((), ())), preferred_elem...  24.5 us
    ppermute x6, waiting for transfers between devices, shifted(): return lax.ppermute(block, axis, route)  23 us
  transfers between devices with their start and end apart: 11, of which 9 were waited for; matrix products, arithmetic and copies ran while one was open for 23% of the time, Pallas kernels for 0%

profile of v1, /device:TPU:1, one launch (start us, length us, event | category | flops | bytes accessed | tf_op | source)
XLA Modules:
  0.0 571.8 jit_solution(3368634060663032119)
XLA Ops:
  7.2 4.4 fusion.195
  13.7 10.1 %all-to-all-start = ((bf16[1,16,9,4096]{3,2,0,1:T(8,128)(2,1)}), bf16[1,16,9,4096]{3,2,0,1:T(8,128)(2,1)}, u32[]{:S(2)}, u32[]{:S(2)}) async-start(bf16[1,16,9,4096]{3,2,0,1:T(8,128)(2,1)} %bitcast.555), calls=%async_computation | async-start | bytes 4194304 | tf_op jit(solution)/shard_map/all_to_all | solution.py:72
  46.1 26.7 %all-to-all-done = bf16[1,16,9,4096]{3,2,0,1:T(8,128)(2,1)} async-done(((bf16[1,16,9,4096]{3,2,0,1:T(8,128)(2,1)}), bf16[1,16,9,4096]{3,2,0,1:T(8,128)(2,1)}, u32[]{:S(2)}, u32[]{:S(2)}) %all-to-all-start) | async-done | bytes 1179680 | tf_op jit(solution)/shard_map/all_to_all | solution.py:72
  72.9 5.0 all-to-all-start.1
  89.3 37.6 %all-to-all-done.1 = bf16[1,16,9,4096]{3,2,0,1:T(8,128)(2,1)} async-done(((bf16[1,16,9,4096]{3,2,0,1:T(8,128)(2,1)}), bf16[1,16,9,4096]{3,2,0,1:T(8,128)(2,1)}, u32[]{:S(2)}, u32[]{:S(2)}) %all-to-all-start.1) | async-done | bytes 1179680 | tf_op jit(solution)/shard_map/all_to_all | solution.py:72
  126.9 5.0 all-to-all-start.2
  142.9 38.1 %all-to-all-done.2 = bf16[1,16,9,4096]{3,2,0,1:T(8,128)(2,1)} async-done(((bf16[1,16,9,4096]{3,2,0,1:T(8,128)(2,1)}), bf16[1,16,9,4096]{3,2,0,1:T(8,128)(2,1)}, u32[]{:S(2)}, u32[]{:S(2)}) %all-to-all-start.2) | async-done | bytes 1179680 | tf_op jit(solution)/shard_map/all_to_all | solution.py:72
  181.0 5.1 all-to-all-start.3
  201.4 33.7 %all-to-all-done.3 = bf16[1,16,9,4096]{3,2,0,1:T(8,128)(2,1)} async-done(((bf16[1,16,9,4096]{3,2,0,1:T(8,128)(2,1)}), bf16[1,16,9,4096]{3,2,0,1:T(8,128)(2,1)}, u32[]{:S(2)}, u32[]{:S(2)}) %all-to-all-start.3) | async-done | bytes 1179680 | tf_op jit(solution)/shard_map/all_to_all | solution.py:72
  240.2 7.0 %dynamic-slice_bitcast_fusion = (bf16[144,4096]{1,0:T(8,128)(2,1)}, bf16[144,4096]{1,0:T(8,128)(2,1)}, bf16[144,4096]{1,0:T(8,128)(2,1)}, bf16[144,4096]{1,0:T(8...) fusion(bf16[4,144,4096]{2,1,0:T(8,128)(2,1)} %constant_dynamic-update-slice_fusion, ...), kind=kLoop, calls=%fused_computation.28 | loop fusion | bytes 16515100 | tf_op jit(solution)/shard_map/jit(dynamic_index_in_dim)/squeeze | solution.py:86
  263.8 4.2 gather_fusion.1
  271.0 4.7 fusion.201
  275.7 4.2 gather_fusion.2
  282.8 4.7 fusion.200
  287.6 4.2 gather_fusion.3
  315.1 4.2 gather_fusion.4
  344.4 4.2 gather_fusion.5
  373.7 5.5 collective-permute-done.3
  389.1 8.5 %collective-permute-done.4 = bf16[48,4096]{1,0:T(8,128)(2,1)S(1)} collective-permute-done((bf16[48,4096]{1,0:T(8,128)(2,1)S(1)}, bf16[48,4096]{1,0:T(8,128)(2,1)S(1)}, u32[]{:S(2)}, u32[]{:S(2)}) %collective-permute-start.4) | collective-permute-done | bytes 393248 | tf_op jit(solution)/shard_map/ppermute | solution.py:18
  416.0 7.1 %collective-permute-done.5 = bf16[48,4096]{1,0:T(8,128)(2,1)S(1)} collective-permute-done((bf16[48,4096]{1,0:T(8,128)(2,1)S(1)}, bf16[48,4096]{1,0:T(8,128)(2,1)S(1)}, u32[]{:S(2)}, u32[]{:S(2)}) %collective-permute-start.5) | collective-permute-done | bytes 393248 | tf_op jit(solution)/shard_map/ppermute | solution.py:18
  436.6 4.2 gather_fusion.6
  453.0 85.4 %all-gather.3.cloned.1.call-done = f32[262144,16]{0,1:T(8,128)} async-done(((f32[4096,16]{0,1:T(8,128)}), f32[262144,16]{0,1:T(8,128)}) %all-gather.3.cloned.1.call-update) | async-done | bytes 16777232 | tf_op jit(solution)/shard_map/all_gather | solution.py:9
  538.4 17.7 %copy.220 = f32[2,8,64,4096]{3,2,1,0:T(8,128)} copy(f32[2,8,64,4096]{3,1,2,0:T(8,128)} %bitcast.552) | data formatting | bytes 33554432
  556.1 8.7 %bitcast_reduce_fusion = f32[4096,16]{0,1:T(8,128)} fusion(f32[2,8,64,4096]{3,2,1,0:T(8,128)} %copy.220), kind=kLoop, calls=%fused_computation.7 | loop fusion | flops 4128768 | bytes 17039360 | tf_op jit(solution)/shard_map/reduce_sum | solution.py:9
  (301 shorter events, 216.4 us)
Async XLA Ops:
  7.2 20.7 %copy-start = (bf16[1,4,48,2,4096]{4,3,2,1,0:T(2,128)(2,1)S(1)}, bf16[1,4,48,2,4096]{4,3,2,1,0:T(2,128)(2,1)}, u32[]{:S(2)}) copy-start(bf16[1,4,48,2,4096]{4,3,2,1,0:T(2,128)(2,1)} %param.7) | copy-start | bytes 9437188
  13.7 10.1 %copy-start.1 = (bf16[1,4096,16]{1,2,0:T(8,128)(2,1)S(1)}, bf16[1,4096,16]{1,2,0:T(8,128)(2,1)}, u32[]{:S(2)}) copy-start(bf16[1,4096,16]{1,2,0:T(8,128)(2,1)} %param.10) | copy-start | bytes 393220
  13.7 12.0 %copy-start.45 = (s32[1,4,48,2]{2,3,1,0:T(2,128)S(1)}, s32[1,4,48,2]{2,3,1,0:T(2,128)}, u32[]{:S(2)}) copy-start(s32[1,4,48,2]{2,3,1,0:T(2,128)} %param.9) | copy-start | bytes 4612
  13.7 59.2 %all-to-all-start = ((bf16[1,16,9,4096]{3,2,0,1:T(8,128)(2,1)}), bf16[1,16,9,4096]{3,2,0,1:T(8,128)(2,1)}, u32[]{:S(2)}, u32[]{:S(2)}) async-start(bf16[1,16,9,4096]{3,2,0,1:T(8,128)(2,1)} %bitcast.555), calls=%async_computation | async-start | bytes 4194304 | tf_op jit(solution)/shard_map/all_to_all | solution.py:72
  44.0 28.9 %copy-start.22 = (s32[48,2]{1,0:T(8,128)}, s32[48,2]{1,0:T(8,128)S(1)}, u32[]{:S(2)}) copy-start(s32[48,2]{1,0:T(8,128)S(1)} %copy.79) | copy-start | bytes 1156
  46.1 31.7 %copy-start.29 = (f32[48,16]{0,1:T(8,128)}, f32[48,16]{0,1:T(8,128)S(1)}, u32[]{:S(2)}) copy-start(f32[48,16]{0,1:T(8,128)S(1)} %get-tuple-element.78) | copy-start | bytes 9220
  46.1 31.7 %copy-start.55 = (f32[48]{0:T(128)}, f32[48]{0:T(128)S(1)}, u32[]{:S(2)}) copy-start(f32[48]{0:T(128)S(1)} %get-tuple-element.77) | copy-start | bytes 580
  72.9 54.0 %all-to-all-start.1 = ((bf16[1,16,9,4096]{3,2,0,1:T(8,128)(2,1)}), bf16[1,16,9,4096]{3,2,0,1:T(8,128)(2,1)}, u32[]{:S(2)}, u32[]{:S(2)}) async-start(bf16[1,16,9,4096]{3,2,0,1:T(8,128)(2,1)} %bitcast.556), calls=%async_computation.1 | async-start | bytes 4194304 | tf_op jit(solution)/shard_map/all_to_all | solution.py:72
  87.2 39.7 %copy-start.17 = (s32[48,2]{1,0:T(8,128)}, s32[48,2]{1,0:T(8,128)S(1)}, u32[]{:S(2)}) copy-start(s32[48,2]{1,0:T(8,128)S(1)} %copy.91) | copy-start | bytes 1156
  89.3 42.6 %copy-start.50 = (f32[48]{0:T(128)}, f32[48]{0:T(128)S(1)}, u32[]{:S(2)}) copy-start(f32[48]{0:T(128)S(1)} %get-tuple-element.93) | copy-start | bytes 580
  126.9 54.0 %all-to-all-start.2 = ((bf16[1,16,9,4096]{3,2,0,1:T(8,128)(2,1)}), bf16[1,16,9,4096]{3,2,0,1:T(8,128)(2,1)}, u32[]{:S(2)}, u32[]{:S(2)}) async-start(bf16[1,16,9,4096]{3,2,0,1:T(8,128)(2,1)} %bitcast.554), calls=%async_computation.2 | async-start | bytes 4194304 | tf_op jit(solution)/shard_map/all_to_all | solution.py:72
  132.1 48.9 %copy-start.16 = (s32[48,2]{1,0:T(8,128)}, s32[48,2]{1,0:T(8,128)S(1)}, u32[]{:S(2)}) copy-start(s32[48,2]{1,0:T(8,128)S(1)} %copy.94) | copy-start | bytes 1156
  181.0 54.2 %all-to-all-start.3 = ((bf16[1,16,9,4096]{3,2,0,1:T(8,128)(2,1)}), bf16[1,16,9,4096]{3,2,0,1:T(8,128)(2,1)}, u32[]{:S(2)}, u32[]{:S(2)}) async-start(bf16[1,16,9,4096]{3,2,0,1:T(8,128)(2,1)} %bitcast.553), calls=%async_computation.3 | async-start | bytes 4194304 | tf_op jit(solution)/shard_map/all_to_all | solution.py:72
  186.1 352.3 %all-gather.3.cloned.1.call-start = ((), (), s32[]{:S(2)}) async-start(), calls=%async_computation.4 | async-start | bytes 17039360 | tf_op jit(solution)/shard_map/all_gather | solution.py:9
  262.1 32.8 %collective-permute-start = (bf16[48,4096]{1,0:T(8,128)(2,1)}, bf16[48,4096]{1,0:T(8,128)(2,1)}, u32[]{:S(2)}, u32[]{:S(2)}) collective-permute-start(bf16[48,4096]{1,0:T(8,128)(2,1)} %get-tuple-element.72), channel_id=1, source_target_pairs={{64,0},{128,64},{192,128},{65,1},{129,65},{193,129},{66,2},{130,66... | collective-permute-start | bytes 1179656 | tf_op jit(solution)/shard_map/ppermute | solution.py:18
  296.1 10.3 %copy-start.32 = (f32[48,16]{0,1:T(8,128)S(1)}, f32[48,16]{0,1:T(8,128)}, u32[]{:S(2)}) copy-start(f32[48,16]{0,1:T(8,128)} %copy-done.31) | copy-start | bytes 9220
  310.9 13.2 %collective-permute-start.1 = (bf16[48,4096]{1,0:T(8,128)(2,1)}, bf16[48,4096]{1,0:T(8,128)(2,1)}, u32[]{:S(2)}, u32[]{:S(2)}) collective-permute-start(bf16[48,4096]{1,0:T(8,128)(2,1)} %get-tuple-element.76), channel_id=1, source_target_pairs={{64,0},{128,64},{192,128},{65,1},{129,65},{193,129},{66,2},{130,66... | collective-permute-start | bytes 1179656 | tf_op jit(solution)/shard_map/ppermute | solution.py:18
  325.2 10.3 %copy-start.30 = (f32[48,16]{0,1:T(8,128)S(1)}, f32[48,16]{0,1:T(8,128)}, u32[]{:S(2)}) copy-start(f32[48,16]{0,1:T(8,128)} %copy-done.29) | copy-start | bytes 9220
  340.1 11.7 %collective-permute-start.2 = (bf16[48,4096]{1,0:T(8,128)(2,1)}, bf16[48,4096]{1,0:T(8,128)(2,1)}, u32[]{:S(2)}, u32[]{:S(2)}) collective-permute-start(bf16[48,4096]{1,0:T(8,128)(2,1)} %get-tuple-element.80), channel_id=1, source_target_pairs={{64,0},{128,64},{192,128},{65,1},{129,65},{193,129},{66,2},{130,66... | collective-permute-start | bytes 1179656 | tf_op jit(solution)/shard_map/ppermute | solution.py:18
  352.9 10.2 %copy-start.28 = (f32[48,16]{0,1:T(8,128)S(1)}, f32[48,16]{0,1:T(8,128)}, u32[]{:S(2)}) copy-start(f32[48,16]{0,1:T(8,128)} %copy-done.27) | copy-start | bytes 9220
  367.5 11.7 %collective-permute-start.3 = (bf16[48,4096]{1,0:T(8,128)(2,1)S(1)}, bf16[48,4096]{1,0:T(8,128)(2,1)S(1)}, u32[]{:S(2)}, u32[]{:S(2)}) collective-permute-start(bf16[48,4096]{1,0:T(8,128)(2,1)S(1)} %get-tuple-element.84), channel_id=1, source_target_pairs={{64,0},{128,64},{192,128},{65,1},{129,65},{193,129},{66,2},{130,66... | collective-permute-start | bytes 1179656 | tf_op jit(solution)/shard_map/ppermute | solution.py:18
  387.4 10.2 %collective-permute-start.4 = (bf16[48,4096]{1,0:T(8,128)(2,1)S(1)}, bf16[48,4096]{1,0:T(8,128)(2,1)S(1)}, u32[]{:S(2)}, u32[]{:S(2)}) collective-permute-start(bf16[48,4096]{1,0:T(8,128)(2,1)S(1)} %get-tuple-element.88), channel_id=1, source_target_pairs={{64,0},{128,64},{192,128},{65,1},{129,65},{193,129},{66,2},{130,66... | collective-permute-start | bytes 1179656 | tf_op jit(solution)/shard_map/ppermute | solution.py:18
  399.4 10.1 %copy-start.24 = (f32[48,16]{0,1:T(8,128)S(1)}, f32[48,16]{0,1:T(8,128)}, u32[]{:S(2)}) copy-start(f32[48,16]{0,1:T(8,128)} %copy-done.23) | copy-start | bytes 9220
  413.9 9.2 %collective-permute-start.5 = (bf16[48,4096]{1,0:T(8,128)(2,1)S(1)}, bf16[48,4096]{1,0:T(8,128)(2,1)S(1)}, u32[]{:S(2)}, u32[]{:S(2)}) collective-permute-start(bf16[48,4096]{1,0:T(8,128)(2,1)S(1)} %get-tuple-element.92), channel_id=1, source_target_pairs={{64,0},{128,64},{192,128},{65,1},{129,65},{193,129},{66,2},{130,66... | collective-permute-start | bytes 1179656 | tf_op jit(solution)/shard_map/ppermute | solution.py:18
  (53 other events, 160.7 us)
Sparse Core Ops, SparseCore 0:
  436.7 101.6 all-gather.2
